TPU v7x, 256 devices: a whole 4x4x8 slice. The times are simulated.
256 devices in a mesh: bits: 64 (over x, z_hi, y, core), freq: 4 (over z_lo).
Axes of the slice: x: 4, y: 4, z: 8 (z_hi: 2, z_lo: 4; z = z_hi * 4 + z_lo), core: 2. Of those that a mesh axis runs over, the one named last changes fastest.
Arguments:
- estimate: float32 [32768, 512], P('bits'), may hold values from -6 to 6
- observed: float32 [4, 32768, 512], P('freq', 'bits'), may hold values from -6 to 6
- factors: float32 [4, 4, 2, 32768, 256], P('freq', None, None, 'bits'), may hold values from -0.25 to 0.25
Outputs:
- updated: float32 [32768, 512], P('bits')
All inputs are finite; a program needn't handle non-finite values.
Results may differ from a plain program's by a relative error of at most 0.00015.
Values sent between devices are 32-bit elements; how exact they have to be, the bound alone decides.
No kernel may reach another device: no remote copies, remote signals or barrier semaphores. Data moves between devices by JAX's collectives and lax.ppermute only.
A program may use at most 64 MiB of HBM per device.

v0:
```python
import jax
import jax.numpy as jnp
from jax import lax
from jax.sharding import PartitionSpec as P


def partner(value, axis, bit):
    mask = 2**bit
    pairs = [(source, source ^ mask) for source in range(lax.axis_size(axis))]
    return lax.ppermute(value, axis, pairs)


def apply_tile(tile_set, field):
    return jnp.einsum("bij,bjs->bis", tile_set, field, precision=lax.Precision.HIGHEST)


def apply_transposed(tile_set, field):
    return jnp.einsum("bji,bjs->bis", tile_set, field, precision=lax.Precision.HIGHEST)


def local(estimate, observed, factors):
    bit_count = lax.axis_size("bits").bit_length() - 1
    levels = factors.shape[1]
    tile_width = factors.shape[-1]
    sources = estimate.shape[1]
    blocks = estimate.shape[0] // tile_width
    shaped = factors[0].reshape(levels, 2, blocks, tile_width, tile_width)
    level_bits = [(bit_count - 1 - level_index) % bit_count for level_index in range(levels)]
    start_field = estimate.reshape(blocks, tile_width, sources)
    observed_field = observed[0].reshape(blocks, tile_width, sources)
    current = start_field
    for level_index in range(levels):
        bit_index = level_bits[level_index]
        partner_field = partner(current, "bits", bit_index)
        current = apply_tile(shaped[level_index, 0], current) + apply_tile(
            shaped[level_index, 1], partner_field
        )
    adjoint = observed_field - current
    for level_index in reversed(range(levels)):
        sent_terms = apply_transposed(shaped[level_index, 1], adjoint)
        arrived = partner(sent_terms, "bits", level_bits[level_index])
        adjoint = apply_transposed(shaped[level_index, 0], adjoint) + arrived
    image_sum = adjoint.reshape(blocks * tile_width, sources)
    gathered = lax.psum(image_sum, "freq")
    return estimate + gathered


def solution(mesh):
    in_specs = (P("bits", None), P("freq", "bits", None), P("freq", None, None, "bits", None))
    out_specs = P("bits", None)
    return jax.shard_map(local, mesh=mesh, in_specs=in_specs, out_specs=out_specs, check_vma=False)
```

profile of v0, /device:TPU:1, one launch (start us, length us, event | category | flops | bytes accessed | tf_op | source)
XLA Modules:
  0.0 336.0 jit_solution(16847460305914774157)
XLA Ops:
  6.5 3.6 %collective-permute-start = (f32[2,256,512]{2,1,0:T(8,128)}, f32[2,256,512]{2,1,0:T(8,128)S(1)}, u32[]{:S(2)}, u32[]{:S(2)}) collective-permute-start(f32[2,256,512]{2,1,0:T(8,128)} %bitcast.98), channel_id=1, source_target_pairs={{0,128},{4,132},{8,136},{12,140},{16,144},{20,148},{24,152},{28,15... | collective-permute-start | bytes 3145736 | tf_op jit(solution)/shard_map/ppermute | solution.py:10
  10.1 2.4 fusion.6
  12.5 19.7 %collective-permute-done = f32[2,256,512]{2,1,0:T(8,128)S(1)} collective-permute-done((f32[2,256,512]{2,1,0:T(8,128)}, f32[2,256,512]{2,1,0:T(8,128)S(1)}, u32[]{:S(2)}, u32[]{:S(2)}) %collective-permute-start) | collective-permute-done | bytes 1048608 | tf_op jit(solution)/shard_map/ppermute | solution.py:10
  32.3 2.1 convolution_add_fusion.3
  34.4 2.2 collective-permute-start.1
  36.5 1.8 fusion.7
  38.4 19.8 %collective-permute-done.1 = f32[2,256,512]{2,1,0:T(8,128)S(1)} collective-permute-done((f32[2,256,512]{2,1,0:T(8,128)S(1)}, f32[2,256,512]{2,1,0:T(8,128)S(1)}, u32[]{:S(2)}, u32[]{:S(2)}) %collective-permute-start.1) | collective-permute-done | bytes 1048608 | tf_op jit(solution)/shard_map/ppermute | solution.py:10
  58.2 1.9 convolution_add_fusion.2
  60.1 7.3 %collective-permute-start.2 = (f32[2,256,512]{1,2,0:T(8,128)S(1)}, f32[2,256,512]{1,2,0:T(8,128)S(1)}, u32[]{:S(2)}, u32[]{:S(2)}) collective-permute-start(f32[2,256,512]{1,2,0:T(8,128)S(1)} %bitcast.102), channel_id=1, source_target_pairs={{0,32},{4,36},{8,40},{12,44},{16,48},{20,52},{24,56},{28,60},{32,0... | collective-permute-start | bytes 3145736 | tf_op jit(solution)/shard_map/ppermute | solution.py:10
  68.4 24.7 %collective-permute-done.2 = f32[2,256,512]{1,2,0:T(8,128)S(1)} collective-permute-done((f32[2,256,512]{1,2,0:T(8,128)S(1)}, f32[2,256,512]{1,2,0:T(8,128)S(1)}, u32[]{:S(2)}, u32[]{:S(2)}) %collective-permute-start.2) | collective-permute-done | bytes 1048608 | tf_op jit(solution)/shard_map/ppermute | solution.py:10
  94.2 3.2 collective-permute-start.3
  97.8 2.3 fusion.9
  100.0 9.7 %collective-permute-done.3 = f32[2,256,512]{1,2,0:T(8,128)} collective-permute-done((f32[2,256,512]{1,2,0:T(8,128)S(1)}, f32[2,256,512]{1,2,0:T(8,128)}, u32[]{:S(2)}, u32[]{:S(2)}) %collective-permute-start.3) | collective-permute-done | bytes 1048608 | tf_op jit(solution)/shard_map/ppermute | solution.py:10
  109.8 2.6 fusion.1
  113.4 3.0 collective-permute-start.4
  116.4 22.9 %collective-permute-done.4 = f32[2,256,512]{1,2,0:T(8,128)S(1)} collective-permute-done((f32[2,256,512]{1,2,0:T(8,128)S(1)}, f32[2,256,512]{1,2,0:T(8,128)S(1)}, u32[]{:S(2)}, u32[]{:S(2)}) %collective-permute-start.4) | collective-permute-done | bytes 1048608 | tf_op jit(solution)/shard_map/ppermute | solution.py:10
  141.6 4.8 %collective-permute-start.5 = (f32[2,256,512]{1,2,0:T(8,128)S(1)}, f32[2,256,512]{1,2,0:T(8,128)S(1)}, u32[]{:S(2)}, u32[]{:S(2)}) collective-permute-start(f32[2,256,512]{1,2,0:T(8,128)S(1)} %convolution_bitcast_fusion.4), channel_id=1, source_target_pairs={{0,32},{4,36},{8,40},{12,44},{16,48},{20,52},{24,56},{28,60},{32,0... | collective-permute-start | bytes 3145736 | tf_op jit(solution)/shard_map/ppermute | solution.py:10
  146.4 12.8 %collective-permute-done.5 = f32[2,256,512]{1,2,0:T(8,128)S(1)} collective-permute-done((f32[2,256,512]{1,2,0:T(8,128)S(1)}, f32[2,256,512]{1,2,0:T(8,128)S(1)}, u32[]{:S(2)}, u32[]{:S(2)}) %collective-permute-start.5) | collective-permute-done | bytes 1048608 | tf_op jit(solution)/shard_map/ppermute | solution.py:10
  162.7 12.7 %collective-permute-done.6 = f32[2,256,512]{1,2,0:T(8,128)S(1)} collective-permute-done((f32[2,256,512]{1,2,0:T(8,128)S(1)}, f32[2,256,512]{1,2,0:T(8,128)S(1)}, u32[]{:S(2)}, u32[]{:S(2)}) %collective-permute-start.6) | collective-permute-done | bytes 1048608 | tf_op jit(solution)/shard_map/ppermute | solution.py:10
  177.7 2.9 collective-permute-start.7
  180.6 12.4 %collective-permute-done.7 = f32[2,256,512]{2,1,0:T(8,128)S(1)} collective-permute-done((f32[2,256,512]{2,1,0:T(8,128)S(1)}, f32[2,256,512]{2,1,0:T(8,128)S(1)}, u32[]{:S(2)}, u32[]{:S(2)}) %collective-permute-start.7) | collective-permute-done | bytes 1048608 | tf_op jit(solution)/shard_map/ppermute | solution.py:10
  193.0 2.2 fusion.2
  195.2 131.6 %all-reduce.2.cloned.1.call-done = f32[512,512]{1,0:T(8,128)} async-done(((f32[512,512]{1,0:T(8,128)}), f32[512,512]{1,0:T(8,128)}) %all-reduce.2.cloned.1.call-update) | async-done | bytes 1048592 | tf_op jit(solution)/shard_map/psum | solution.py:44
  326.8 2.4 add.49
  (21 shorter events, 11.6 us)
Async XLA Ops:
  6.5 320.3 %all-reduce.2.cloned.1.call-start = ((), (), s32[]{:S(2)}) async-start(), calls=%async_computation | async-start | bytes 2097152 | tf_op jit(solution)/shard_map/psum | solution.py:44
  6.5 30.0 %copy-start = (f32[1,4,2,512,256]{4,3,2,1,0:T(8,128)S(1)}, f32[1,4,2,512,256]{4,3,2,1,0:T(8,128)}, u32[]{:S(2)}) copy-start(f32[1,4,2,512,256]{4,3,2,1,0:T(8,128)} %param.5) | copy-start | bytes 12582916
  6.5 25.7 %collective-permute-start = (f32[2,256,512]{2,1,0:T(8,128)}, f32[2,256,512]{2,1,0:T(8,128)S(1)}, u32[]{:S(2)}, u32[]{:S(2)}) collective-permute-start(f32[2,256,512]{2,1,0:T(8,128)} %bitcast.98), channel_id=1, source_target_pairs={{0,128},{4,132},{8,136},{12,140},{16,144},{20,148},{24,152},{28,15... | collective-permute-start | bytes 3145736 | tf_op jit(solution)/shard_map/ppermute | solution.py:10
  34.4 23.9 %collective-permute-start.1 = (f32[2,256,512]{2,1,0:T(8,128)S(1)}, f32[2,256,512]{2,1,0:T(8,128)S(1)}, u32[]{:S(2)}, u32[]{:S(2)}) collective-permute-start(f32[2,256,512]{2,1,0:T(8,128)S(1)} %convolution_add_fusion.3), channel_id=1, source_target_pairs={{0,64},{4,68},{8,72},{12,76},{16,80},{20,84},{24,88},{28,92},{32,9... | collective-permute-start | bytes 3145736 | tf_op jit(solution)/shard_map/ppermute | solution.py:10
  38.4 59.0 %copy-start.3 = (f32[1,512,512]{2,1,0:T(8,128)S(1)}, f32[1,512,512]{2,1,0:T(8,128)}, u32[]{:S(2)}) copy-start(f32[1,512,512]{2,1,0:T(8,128)} %param.4) | copy-start | bytes 3145732
  60.1 33.1 %collective-permute-start.2 = (f32[2,256,512]{1,2,0:T(8,128)S(1)}, f32[2,256,512]{1,2,0:T(8,128)S(1)}, u32[]{:S(2)}, u32[]{:S(2)}) collective-permute-start(f32[2,256,512]{1,2,0:T(8,128)S(1)} %bitcast.102), channel_id=1, source_target_pairs={{0,32},{4,36},{8,40},{12,44},{16,48},{20,52},{24,56},{28,60},{32,0... | collective-permute-start | bytes 3145736 | tf_op jit(solution)/shard_map/ppermute | solution.py:10
  94.2 15.5 %collective-permute-start.3 = (f32[2,256,512]{1,2,0:T(8,128)S(1)}, f32[2,256,512]{1,2,0:T(8,128)}, u32[]{:S(2)}, u32[]{:S(2)}) collective-permute-start(f32[2,256,512]{1,2,0:T(8,128)S(1)} %bitcast.101), channel_id=1, source_target_pairs={{0,16},{4,20},{8,24},{12,28},{16,0},{20,4},{24,8},{28,12},{32,48},... | collective-permute-start | bytes 3145736 | tf_op jit(solution)/shard_map/ppermute | solution.py:10
  97.8 14.6 %copy-start.1 = (f32[1,4,2,512,256]{4,3,2,1,0:T(8,128)S(1)}, f32[1,4,2,512,256]{4,3,2,1,0:T(8,128)}, u32[]{:S(2)}) copy-start(f32[1,4,2,512,256]{4,3,2,1,0:T(8,128)} %param.5) | copy-start | bytes 12582916
  113.4 25.9 %collective-permute-start.4 = (f32[2,256,512]{1,2,0:T(8,128)S(1)}, f32[2,256,512]{1,2,0:T(8,128)S(1)}, u32[]{:S(2)}, u32[]{:S(2)}) collective-permute-start(f32[2,256,512]{1,2,0:T(8,128)S(1)} %convolution_bitcast_fusion.6), channel_id=1, source_target_pairs={{0,16},{4,20},{8,24},{12,28},{16,0},{20,4},{24,8},{28,12},{32,48},... | collective-permute-start | bytes 3145736 | tf_op jit(solution)/shard_map/ppermute | solution.py:10
  141.6 17.6 %collective-permute-start.5 = (f32[2,256,512]{1,2,0:T(8,128)S(1)}, f32[2,256,512]{1,2,0:T(8,128)S(1)}, u32[]{:S(2)}, u32[]{:S(2)}) collective-permute-start(f32[2,256,512]{1,2,0:T(8,128)S(1)} %convolution_bitcast_fusion.4), channel_id=1, source_target_pairs={{0,32},{4,36},{8,40},{12,44},{16,48},{20,52},{24,56},{28,60},{32,0... | collective-permute-start | bytes 3145736 | tf_op jit(solution)/shard_map/ppermute | solution.py:10
  161.4 14.0 %collective-permute-start.6 = (f32[2,256,512]{1,2,0:T(8,128)S(1)}, f32[2,256,512]{1,2,0:T(8,128)S(1)}, u32[]{:S(2)}, u32[]{:S(2)}) collective-permute-start(f32[2,256,512]{1,2,0:T(8,128)S(1)} %convolution_bitcast_fusion.2), channel_id=1, source_target_pairs={{0,64},{4,68},{8,72},{12,76},{16,80},{20,84},{24,88},{28,92},{32,9... | collective-permute-start | bytes 3145736 | tf_op jit(solution)/shard_map/ppermute | solution.py:10
  176.6 150.2 %copy-start.2 = (f32[512,512]{1,0:T(8,128)S(1)}, f32[512,512]{1,0:T(8,128)}, u32[]{:S(2)}) copy-start(f32[512,512]{1,0:T(8,128)} %param.3) | copy-start | bytes 3145732
  177.7 15.2 %collective-permute-start.7 = (f32[2,256,512]{2,1,0:T(8,128)S(1)}, f32[2,256,512]{2,1,0:T(8,128)S(1)}, u32[]{:S(2)}, u32[]{:S(2)}) collective-permute-start(f32[2,256,512]{2,1,0:T(8,128)S(1)} %convolution_bitcast_fusion), channel_id=1, source_target_pairs={{0,128},{4,132},{8,136},{12,140},{16,144},{20,148},{24,152},{28,15... | collective-permute-start | bytes 3145736 | tf_op jit(solution)/shard_map/ppermute | solution.py:10
Sparse Core Ops, SparseCore 0:
  195.3 131.4 all-reduce.1
where the time goes:
time: 336 us
  waiting for transfers between devices  266 us (79%)
  starting transfers between devices  28.2 us (8%)
  matrix products  25.2 us (8%)
  between operations  13.6 us (4%)
    ppermute x8, waiting for transfers between devices, partner(): return lax.ppermute(value, axis, pairs)  135 us
    psum x1, waiting for transfers between devices, local(): gathered = lax.psum(image_sum, 'freq')  132 us
    ppermute x8, starting transfers between devices, partner(): return lax.ppermute(value, axis, pairs)  28.2 us
    dot_general x8, matrix products, apply_tile(): jnp.einsum('bij,bjs->bis', tile_set, field, precision=lax.Precision.HIGHEST)  15.2 us
    dot_general x8, matrix products, apply_transposed(): jnp.einsum('bji,bjs->bis', tile_set, field, precision=lax.Precision.HIGHEST)  9.95 us
  transfers between devices with their start and end apart: 9, of which 9 were waited for; matrix products, arithmetic and copies ran while one was open for 2% of the time, Pallas kernels for 0%

commit v1 on v0

--- a/solution.py
+++ b/solution.py
@@ -41,7 +41,7 @@
         arrived = partner(sent_terms, "bits", level_bits[level_index])
         adjoint = apply_transposed(shaped[level_index, 0], adjoint) + arrived
     image_sum = adjoint.reshape(blocks * tile_width, sources)
-    gathered = lax.psum(image_sum, "freq")
+    gathered = jnp.sum(lax.all_gather(image_sum, "freq"), axis=0)
     return estimate + gathered
 
 

time: 336 us -> 358 us (1.065)
  waiting for transfers between devices: 266 us -> 287 us
    all_gather x0 -> x1, waiting for transfers between devices: none -> 152 us  [local(): gathered = jnp.sum(lax.all_gather(image_sum, 'freq'), axis=0)]
    psum x1 -> x0, waiting for transfers between devices: 132 us -> none  [local(): gathered = lax.psum(image_sum, 'freq')]
where the time goes in v1:
time: 358 us
  waiting for transfers between devices  287 us (80%)
  starting transfers between devices  28.2 us (8%)
  matrix products  25.2 us (7%)
  between operations  13.6 us (4%)
  other arithmetic  3.95 us (1%)
    all_gather x1, waiting for transfers between devices, local(): gathered = jnp.sum(lax.all_gather(image_sum, 'freq'), axis=0)  152 us
    ppermute x8, waiting for transfers between devices, partner(): return lax.ppermute(value, axis, pairs)  135 us
    ppermute x8, starting transfers between devices, partner(): return lax.ppermute(value, axis, pairs)  28.2 us
    dot_general x8, matrix products, apply_tile(): jnp.einsum('bij,bjs->bis', tile_set, field, precision=lax.Precision.HIGHEST)  15.2 us
    dot_general x8, matrix products, apply_transposed(): jnp.einsum('bji,bjs->bis', tile_set, field, precision=lax.Precision.HIGHEST)  9.94 us
  transfers between devices with their start and end apart: 9, of which 9 were waited for; matrix products, arithmetic and copies ran while one was open for 2% of the time, Pallas kernels for 0%

profile of v1, /device:TPU:1, one launch (start us, length us, event | category | flops | bytes accessed | tf_op | source)
XLA Modules:
  0.0 358.0 jit_solution(4586473933812978643)
XLA Ops:
  6.5 3.6 collective-permute-start
  10.1 2.4 fusion.6
  12.5 19.7 %collective-permute-done = f32[2,256,512]{2,1,0:T(8,128)S(1)} collective-permute-done((f32[2,256,512]{2,1,0:T(8,128)}, f32[2,256,512]{2,1,0:T(8,128)S(1)}, u32[]{:S(2)}, u32[]{:S(2)}) %collective-permute-start) | collective-permute-done | bytes 1048608 | tf_op jit(solution)/shard_map/ppermute | solution.py:10
  32.3 2.1 convolution_add_fusion.3
  34.4 2.2 collective-permute-start.1
  36.5 1.8 fusion.7
  38.4 19.8 %collective-permute-done.1 = f32[2,256,512]{2,1,0:T(8,128)S(1)} collective-permute-done((f32[2,256,512]{2,1,0:T(8,128)S(1)}, f32[2,256,512]{2,1,0:T(8,128)S(1)}, u32[]{:S(2)}, u32[]{:S(2)}) %collective-permute-start.1) | collective-permute-done | bytes 1048608 | tf_op jit(solution)/shard_map/ppermute | solution.py:10
  58.2 1.9 convolution_add_fusion.2
  60.1 7.3 %collective-permute-start.2 = (f32[2,256,512]{1,2,0:T(8,128)S(1)}, f32[2,256,512]{1,2,0:T(8,128)S(1)}, u32[]{:S(2)}, u32[]{:S(2)}) collective-permute-start(f32[2,256,512]{1,2,0:T(8,128)S(1)} %bitcast.102), channel_id=1, source_target_pairs={{0,32},{4,36},{8,40},{12,44},{16,48},{20,52},{24,56},{28,60},{32,0... | collective-permute-start | bytes 3145736 | tf_op jit(solution)/shard_map/ppermute | solution.py:10
  68.4 24.7 %collective-permute-done.2 = f32[2,256,512]{1,2,0:T(8,128)S(1)} collective-permute-done((f32[2,256,512]{1,2,0:T(8,128)S(1)}, f32[2,256,512]{1,2,0:T(8,128)S(1)}, u32[]{:S(2)}, u32[]{:S(2)}) %collective-permute-start.2) | collective-permute-done | bytes 1048608 | tf_op jit(solution)/shard_map/ppermute | solution.py:10
  94.2 3.2 collective-permute-start.3
  97.8 2.3 fusion.9
  100.0 9.7 %collective-permute-done.3 = f32[2,256,512]{1,2,0:T(8,128)} collective-permute-done((f32[2,256,512]{1,2,0:T(8,128)S(1)}, f32[2,256,512]{1,2,0:T(8,128)}, u32[]{:S(2)}, u32[]{:S(2)}) %collective-permute-start.3) | collective-permute-done | bytes 1048608 | tf_op jit(solution)/shard_map/ppermute | solution.py:10
  109.8 2.6 fusion.1
  113.4 3.0 collective-permute-start.4
  116.4 22.9 %collective-permute-done.4 = f32[2,256,512]{1,2,0:T(8,128)S(1)} collective-permute-done((f32[2,256,512]{1,2,0:T(8,128)S(1)}, f32[2,256,512]{1,2,0:T(8,128)S(1)}, u32[]{:S(2)}, u32[]{:S(2)}) %collective-permute-start.4) | collective-permute-done | bytes 1048608 | tf_op jit(solution)/shard_map/ppermute | solution.py:10
  141.6 4.8 %collective-permute-start.5 = (f32[2,256,512]{1,2,0:T(8,128)S(1)}, f32[2,256,512]{1,2,0:T(8,128)S(1)}, u32[]{:S(2)}, u32[]{:S(2)}) collective-permute-start(f32[2,256,512]{1,2,0:T(8,128)S(1)} %convolution_bitcast_fusion.4), channel_id=1, source_target_pairs={{0,32},{4,36},{8,40},{12,44},{16,48},{20,52},{24,56},{28,60},{32,0... | collective-permute-start | bytes 3145736 | tf_op jit(solution)/shard_map/ppermute | solution.py:10
  146.4 12.8 %collective-permute-done.5 = f32[2,256,512]{1,2,0:T(8,128)S(1)} collective-permute-done((f32[2,256,512]{1,2,0:T(8,128)S(1)}, f32[2,256,512]{1,2,0:T(8,128)S(1)}, u32[]{:S(2)}, u32[]{:S(2)}) %collective-permute-start.5) | collective-permute-done | bytes 1048608 | tf_op jit(solution)/shard_map/ppermute | solution.py:10
  162.7 12.7 %collective-permute-done.6 = f32[2,256,512]{1,2,0:T(8,128)S(1)} collective-permute-done((f32[2,256,512]{1,2,0:T(8,128)S(1)}, f32[2,256,512]{1,2,0:T(8,128)S(1)}, u32[]{:S(2)}, u32[]{:S(2)}) %collective-permute-start.6) | collective-permute-done | bytes 1048608 | tf_op jit(solution)/shard_map/ppermute | solution.py:10
  177.7 2.9 collective-permute-start.7
  180.6 12.4 %collective-permute-done.7 = f32[2,256,512]{2,1,0:T(8,128)S(1)} collective-permute-done((f32[2,256,512]{2,1,0:T(8,128)S(1)}, f32[2,256,512]{2,1,0:T(8,128)S(1)}, u32[]{:S(2)}, u32[]{:S(2)}) %collective-permute-start.7) | collective-permute-done | bytes 1048608 | tf_op jit(solution)/shard_map/ppermute | solution.py:10
  193.0 2.2 fusion.2
  195.2 152.0 %all-gather.2.cloned.1.call-done = f32[4,512,512]{2,1,0:T(8,128)} async-done(((f32[1,512,512]{2,1,0:T(8,128)}), f32[4,512,512]{2,1,0:T(8,128)}) %all-gather.2.cloned.1.call-update) | async-done | bytes 4194320 | tf_op jit(solution)/shard_map/all_gather | solution.py:44
  347.2 2.8 reduce_sum.9
  (22 shorter events, 12.8 us)
Async XLA Ops:
  6.5 340.6 %all-gather.2.cloned.1.call-start = ((), (), s32[]{:S(2)}) async-start(), calls=%async_computation | async-start | bytes 5242880 | tf_op jit(solution)/shard_map/all_gather | solution.py:44
  6.5 30.0 %copy-start = (f32[1,4,2,512,256]{4,3,2,1,0:T(8,128)S(1)}, f32[1,4,2,512,256]{4,3,2,1,0:T(8,128)}, u32[]{:S(2)}) copy-start(f32[1,4,2,512,256]{4,3,2,1,0:T(8,128)} %param.5) | copy-start | bytes 12582916
  6.5 25.7 %collective-permute-start = (f32[2,256,512]{2,1,0:T(8,128)}, f32[2,256,512]{2,1,0:T(8,128)S(1)}, u32[]{:S(2)}, u32[]{:S(2)}) collective-permute-start(f32[2,256,512]{2,1,0:T(8,128)} %bitcast.98), channel_id=1, source_target_pairs={{0,128},{4,132},{8,136},{12,140},{16,144},{20,148},{24,152},{28,15... | collective-permute-start | bytes 3145736 | tf_op jit(solution)/shard_map/ppermute | solution.py:10
  34.4 23.9 %collective-permute-start.1 = (f32[2,256,512]{2,1,0:T(8,128)S(1)}, f32[2,256,512]{2,1,0:T(8,128)S(1)}, u32[]{:S(2)}, u32[]{:S(2)}) collective-permute-start(f32[2,256,512]{2,1,0:T(8,128)S(1)} %convolution_add_fusion.3), channel_id=1, source_target_pairs={{0,64},{4,68},{8,72},{12,76},{16,80},{20,84},{24,88},{28,92},{32,9... | collective-permute-start | bytes 3145736 | tf_op jit(solution)/shard_map/ppermute | solution.py:10
  38.4 59.0 %copy-start.3 = (f32[1,512,512]{2,1,0:T(8,128)S(1)}, f32[1,512,512]{2,1,0:T(8,128)}, u32[]{:S(2)}) copy-start(f32[1,512,512]{2,1,0:T(8,128)} %param.4) | copy-start | bytes 3145732
  60.1 33.1 %collective-permute-start.2 = (f32[2,256,512]{1,2,0:T(8,128)S(1)}, f32[2,256,512]{1,2,0:T(8,128)S(1)}, u32[]{:S(2)}, u32[]{:S(2)}) collective-permute-start(f32[2,256,512]{1,2,0:T(8,128)S(1)} %bitcast.102), channel_id=1, source_target_pairs={{0,32},{4,36},{8,40},{12,44},{16,48},{20,52},{24,56},{28,60},{32,0... | collective-permute-start | bytes 3145736 | tf_op jit(solution)/shard_map/ppermute | solution.py:10
  94.2 15.5 %collective-permute-start.3 = (f32[2,256,512]{1,2,0:T(8,128)S(1)}, f32[2,256,512]{1,2,0:T(8,128)}, u32[]{:S(2)}, u32[]{:S(2)}) collective-permute-start(f32[2,256,512]{1,2,0:T(8,128)S(1)} %bitcast.101), channel_id=1, source_target_pairs={{0,16},{4,20},{8,24},{12,28},{16,0},{20,4},{24,8},{28,12},{32,48},... | collective-permute-start | bytes 3145736 | tf_op jit(solution)/shard_map/ppermute | solution.py:10
  97.8 14.6 %copy-start.1 = (f32[1,4,2,512,256]{4,3,2,1,0:T(8,128)S(1)}, f32[1,4,2,512,256]{4,3,2,1,0:T(8,128)}, u32[]{:S(2)}) copy-start(f32[1,4,2,512,256]{4,3,2,1,0:T(8,128)} %param.5) | copy-start | bytes 12582916
  113.4 25.9 %collective-permute-start.4 = (f32[2,256,512]{1,2,0:T(8,128)S(1)}, f32[2,256,512]{1,2,0:T(8,128)S(1)}, u32[]{:S(2)}, u32[]{:S(2)}) collective-permute-start(f32[2,256,512]{1,2,0:T(8,128)S(1)} %convolution_bitcast_fusion.6), channel_id=1, source_target_pairs={{0,16},{4,20},{8,24},{12,28},{16,0},{20,4},{24,8},{28,12},{32,48},... | collective-permute-start | bytes 3145736 | tf_op jit(solution)/shard_map/ppermute | solution.py:10
  141.6 17.6 %collective-permute-start.5 = (f32[2,256,512]{1,2,0:T(8,128)S(1)}, f32[2,256,512]{1,2,0:T(8,128)S(1)}, u32[]{:S(2)}, u32[]{:S(2)}) collective-permute-start(f32[2,256,512]{1,2,0:T(8,128)S(1)} %convolution_bitcast_fusion.4), channel_id=1, source_target_pairs={{0,32},{4,36},{8,40},{12,44},{16,48},{20,52},{24,56},{28,60},{32,0... | collective-permute-start | bytes 3145736 | tf_op jit(solution)/shard_map/ppermute | solution.py:10
  161.4 14.0 %collective-permute-start.6 = (f32[2,256,512]{1,2,0:T(8,128)S(1)}, f32[2,256,512]{1,2,0:T(8,128)S(1)}, u32[]{:S(2)}, u32[]{:S(2)}) collective-permute-start(f32[2,256,512]{1,2,0:T(8,128)S(1)} %convolution_bitcast_fusion.2), channel_id=1, source_target_pairs={{0,64},{4,68},{8,72},{12,76},{16,80},{20,84},{24,88},{28,92},{32,9... | collective-permute-start | bytes 3145736 | tf_op jit(solution)/shard_map/ppermute | solution.py:10
  177.7 172.2 %copy-start.2 = (f32[512,512]{1,0:T(8,128)S(1)}, f32[512,512]{1,0:T(8,128)}, u32[]{:S(2)}) copy-start(f32[512,512]{1,0:T(8,128)} %param.3) | copy-start | bytes 3145732
  177.7 15.2 %collective-permute-start.7 = (f32[2,256,512]{2,1,0:T(8,128)S(1)}, f32[2,256,512]{2,1,0:T(8,128)S(1)}, u32[]{:S(2)}, u32[]{:S(2)}) collective-permute-start(f32[2,256,512]{2,1,0:T(8,128)S(1)} %convolution_bitcast_fusion), channel_id=1, source_target_pairs={{0,128},{4,132},{8,136},{12,140},{16,144},{20,148},{24,152},{28,15... | collective-permute-start | bytes 3145736 | tf_op jit(solution)/shard_map/ppermute | solution.py:10
Sparse Core Ops, SparseCore 0:
  195.3 151.8 all-gather.1
